TPU v7x, 32 devices: a whole 2x2x4 slice. The times are simulated.
32 devices in a mesh: dp: 2 (over core), row: 4 (over y, x), col: 4 (over z).
Axes of the slice: x: 2, y: 2, z: 4, core: 2. Of those that a mesh axis runs over, the one named last changes fastest.
Arguments:
- hidden: bfloat16 [2048, 1024], P(('dp', 'row')), may hold values from -6 to 6
- segments: int32 [2, 1024], P('dp'), may hold values from 0 to 3, never falling along the last dimension, each value on 1 to 512 neighbouring positions
- cotangent: bfloat16 [2048, 1024], P(('dp', 'row')), may hold values from -6 to 6
- norm_gain: float32 [2, 1024], replicated, may hold values from 0.5 to 1.5
- zx_weight: bfloat16 [2, 1024, 4096], P(None, 'col', 'row'), may hold values from -0.1875 to 0.1875
- dt_weight: bfloat16 [2, 1024, 32], P(None, 'col', 'row'), may hold values from -0.1875 to 0.1875
- bc_weight: bfloat16 [2, 1024, 256], replicated, may hold values from -0.1875 to 0.1875
- conv_x: float32 [2, 4, 2048], P(None, None, ('row', 'col')), may hold values from -3 to 3
- conv_x_bias: float32 [2, 2048], P(None, ('row', 'col')), may hold values from -3 to 3
- conv_bc: float32 [2, 4, 256], replicated, may hold values from -3 to 3
- conv_bc_bias: float32 [2, 256], replicated, may hold values from -3 to 3
- dt_bias: float32 [2, 32], P(None, ('row', 'col')), may hold values from -6 to -2
- a_log: float32 [2, 32], P(None, ('row', 'col')), may hold values from -2 to 2.5
- skip_d: float32 [2, 32], P(None, ('row', 'col')), may hold values from 0.5 to 1.5
- gnorm_gain: float32 [2, 2048], P(None, ('row', 'col')), may hold values from 0.5 to 1.5
- out_weight: bfloat16 [2, 2048, 1024], P(None, ('row', 'col')), may hold values from -0.125 to 0.125
Outputs:
- hidden_out: bfloat16 [2048, 1024], P(('dp', 'row'))
- d_hidden: float32 [2048, 1024], P(('dp', 'row'))
- d_norm_gain: float32 [2, 1024], replicated
- d_zx_weight: float32 [2, 1024, 4096], P(None, 'col', 'row')
- d_dt_weight: float32 [2, 1024, 32], P(None, 'col', 'row')
- d_bc_weight: float32 [2, 1024, 256], replicated
- d_conv_x: float32 [2, 4, 2048], P(None, None, ('row', 'col'))
- d_conv_x_bias: float32 [2, 2048], P(None, ('row', 'col'))
- d_conv_bc: float32 [2, 4, 256], replicated
- d_conv_bc_bias: float32 [2, 256], replicated
- d_dt_bias: float32 [2, 32], P(None, ('row', 'col'))
- d_a_log: float32 [2, 32], P(None, ('row', 'col'))
- d_skip_d: float32 [2, 32], P(None, ('row', 'col'))
- d_gnorm_gain: float32 [2, 2048], P(None, ('row', 'col'))
- d_out_weight: float32 [2, 2048, 1024], P(None, ('row', 'col'))
Inputs may be any that keep to these rules, and one draw needn't show every extreme that they name: `segments`: within a sequence the document numbers never fall; each document is a run of 1 to 512 tokens, and in every sequence one document has exactly 512 tokens.
All inputs are finite; a program needn't handle non-finite values.
Results may differ from a plain program's by a relative error of at most 0.04.
Values may be sent and summed in bfloat16 or wider, within the bound.
No kernel may reach another device: no remote copies, remote signals or barrier semaphores. Data moves between devices by JAX's collectives and lax.ppermute only.
A program may use at most 128 MiB of HBM per device.

v0:
```python
from functools import partial
import jax
import jax.numpy as jnp
from jax import lax
from jax.sharding import PartitionSpec as P

HEADS = 32
HEAD_DIM = 64
BLOCK = 256
EPS = 1e-05
HIGHEST = lax.Precision.HIGHEST
CONTRACT_ROWS = (((0,), (0,)), ((), ()))
CONTRACT_COLS = (((1,), (1,)), ((), ()))


def shortened(array):

    def short(part):
        return part.astype(jnp.bfloat16) if part.dtype == jnp.float32 else part

    return jax.tree.map(short, array)


def conv_masks(seg_ids, taps):
    seg_masks = [jnp.ones(seg_ids.shape, jnp.float32)]
    for offset in range(1, taps):
        earlier = jnp.concatenate(
            [jnp.full((seg_ids.shape[0], offset), -1, jnp.int32), seg_ids[:, :-offset]], axis=1
        )
        seg_masks.append((earlier == seg_ids).astype(jnp.float32))
    return seg_masks


def causal_conv(values, kernel, conv_bias, seg_masks):
    running = conv_bias + kernel[0] * values
    for offset in range(1, kernel.shape[0]):
        padding = jnp.zeros((values.shape[0], offset, values.shape[2]), jnp.float32)
        shifted = jnp.concatenate([padding, values[:, :-offset]], axis=1)
        running = running + kernel[offset] * shifted * seg_masks[offset][:, :, None]
    return running


def mixer_piece(
    seg_ids,
    block,
    mixed_in,
    step_in,
    side_in,
    conv_x,
    conv_x_bias,
    conv_bc,
    conv_bc_bias,
    dt_bias,
    a_log,
    skip_d,
):
    seq_count, length = seg_ids.shape
    heads = step_in.shape[1]
    head_dim = mixed_in.shape[1] // (2 * heads)
    state = side_in.shape[1] // 2
    blocks = length // block
    seg_masks = conv_masks(seg_ids, conv_x.shape[0])
    halves = mixed_in.reshape(seq_count, length, heads, 2, head_dim)
    gate_in = halves[:, :, :, 0, :]
    values = halves[:, :, :, 1, :].reshape(seq_count, length, heads * head_dim)
    values = jax.nn.silu(causal_conv(values, conv_x, conv_x_bias, seg_masks))
    side = jax.nn.silu(
        causal_conv(side_in.reshape(seq_count, length, 2 * state), conv_bc, conv_bc_bias, seg_masks)
    )
    steps = jax.nn.softplus(step_in.reshape(seq_count, length, heads) + dt_bias)
    layout = (seq_count, blocks, block)
    inputs = side[:, :, :state].reshape(layout + (state,))
    readout = side[:, :, state:].reshape(layout + (state,))
    sources = values.reshape(layout + (heads, head_dim))
    steps_head = steps.reshape(layout + (heads,)).transpose(0, 1, 3, 2)
    decays = jnp.cumsum(steps_head * (-jnp.exp(a_log))[:, None], axis=3)
    seg_layout = seg_ids.reshape(layout)
    places = jnp.arange(block)
    causal = places[:, None] >= places[None, :]
    allowed = (seg_layout[:, :, :, None] == seg_layout[:, :, None, :]) & causal
    spans = decays[:, :, :, :, None] - decays[:, :, :, None, :]
    weights = jnp.exp(jnp.where(allowed[:, :, None], spans, -1e30))
    affinity = jnp.einsum("scqn,sckn->scqk", readout, inputs, precision=HIGHEST)
    scores = affinity[:, :, None] * weights * steps_head[:, :, :, None, :]
    result = jnp.einsum("schqk,sckhp->scqhp", scores, sources, precision=HIGHEST)
    last_seg = seg_layout[:, :, -1]
    same_last = (seg_layout == last_seg[:, :, None]).astype(jnp.float32)
    to_end = jnp.exp(decays[:, :, :, -1:] - decays) * same_last[:, :, None, :] * steps_head
    scaled = sources * to_end.transpose(0, 1, 3, 2)[..., None]
    states = jnp.einsum("sckn,sckhp->schnp", inputs, scaled, precision=HIGHEST)
    carried = states[:, 0]
    outputs = [jnp.zeros((seq_count, block, heads, head_dim), jnp.float32)]
    for index in range(1, blocks):
        keeper = (seg_layout[:, index] == last_seg[:, index - 1][:, None]).astype(jnp.float32)
        factor = jnp.exp(decays[:, index]) * keeper[:, None, :]
        earlier = jnp.einsum("sqn,shnp->sqhp", readout[:, index], carried, precision=HIGHEST)
        outputs.append(earlier * factor.transpose(0, 2, 1)[..., None])
        if index + 1 < blocks:
            linked = (last_seg[:, index] == last_seg[:, index - 1]).astype(jnp.float32)
            carry_decay = jnp.exp(decays[:, index, :, -1]) * linked[:, None]
            carried = states[:, index] + carry_decay[:, :, None, None] * carried
    result = result + jnp.stack(outputs, axis=1) + skip_d[:, None] * sources
    gated = result.reshape(seq_count, length, heads, head_dim) * jax.nn.silu(gate_in)
    return gated.reshape(seq_count * length, heads * head_dim)


def total_heads(terms):
    return jax.tree.map(lambda part: part.astype(jnp.float32), lax.psum(shortened(terms), "dp"))


def total_shared(terms):
    return lax.psum(terms, ("dp", "row", "col"))


def shards(
    hidden,
    segments,
    cotangent,
    norm_gain,
    zx_weight,
    dt_weight,
    bc_weight,
    conv_x,
    conv_x_bias,
    conv_bc,
    conv_bc_bias,
    dt_bias,
    a_log,
    skip_d,
    gnorm_gain,
    out_weight,
):
    col_count = lax.axis_size("col")
    row_count_axis = lax.axis_size("row")
    col_index = lax.axis_index("col")
    width = hidden.shape[1]
    col_width = width // col_count
    layers = zx_weight.shape[0]
    state_width = bc_weight.shape[2]
    inner_total = HEADS * HEAD_DIM
    rows_here = hidden.shape[0]
    resid = hidden.astype(jnp.float32)
    stored = []
    for layer_index in range(layers):
        scale = lax.rsqrt(jnp.mean(resid * resid, axis=1, keepdims=True) + EPS)
        normed = (resid * scale * norm_gain[layer_index]).astype(jnp.bfloat16)
        side = jnp.dot(normed, bc_weight[layer_index], preferred_element_type=jnp.float32).astype(
            jnp.bfloat16
        )
        normed_cols = lax.dynamic_slice_in_dim(normed, col_index * col_width, col_width, 1)
        gathered_cols, side_all = (
            lax.all_gather(normed_cols, "row", axis=0, tiled=True),
            lax.all_gather(side, "row", axis=0, tiled=True),
        )
        part_mixed = jnp.dot(
            gathered_cols, zx_weight[layer_index], preferred_element_type=jnp.float32
        )
        part_steps = jnp.dot(
            gathered_cols, dt_weight[layer_index], preferred_element_type=jnp.float32
        )
        mixed_sum, step_sum = (
            lax.psum_scatter(part_mixed, "col", scatter_dimension=1, tiled=True),
            lax.psum_scatter(part_steps, "col", scatter_dimension=1, tiled=True),
        )
        mixed_in = mixed_sum.astype(jnp.bfloat16)
        step_in = step_sum.astype(jnp.bfloat16)
        piece = partial(mixer_piece, segments, BLOCK)
        gated, pullback = jax.vjp(
            piece,
            mixed_in.astype(jnp.float32),
            step_in.astype(jnp.float32),
            side_all.astype(jnp.float32),
            conv_x[layer_index],
            conv_x_bias[layer_index],
            conv_bc[layer_index],
            conv_bc_bias[layer_index],
            dt_bias[layer_index],
            a_log[layer_index],
            skip_d[layer_index],
        )
        squares = lax.psum(jnp.sum(gated * gated, axis=1), ("row", "col"))
        inverse = lax.rsqrt(squares / inner_total + EPS)[:, None]
        normed_out = (gated * inverse * gnorm_gain[layer_index]).astype(jnp.bfloat16)

        def project(first_row, row_count, source=normed_out, weight=out_weight[layer_index]):
            return jnp.dot(source, weight, preferred_element_type=jnp.float32)

        kept_rows = normed_out.shape[0] // (row_count_axis * col_count)
        shared_rows = lax.psum_scatter(
            project(jnp.int32(0), lax.axis_size(("row", "col")) * kept_rows),
            ("row", "col"),
            scatter_dimension=0,
            tiled=True,
        )
        branch = lax.all_gather(shared_rows, "col", axis=0, tiled=True)
        stored.append((resid, scale, normed, gathered_cols, gated, inverse, normed_out, pullback))
        resid = resid + branch
    result_out = resid.astype(jnp.bfloat16)
    grad = cotangent.astype(jnp.float32)
    heads_terms = [None] * layers
    shared_terms = [None] * layers
    for layer_index in reversed(range(layers)):
        resid_in, scale, normed, gathered_cols, gated, inverse, normed_out, pullback = stored[
            layer_index
        ]
        grad_low = grad.astype(jnp.bfloat16)
        grad_full = lax.all_gather(grad_low, "row", axis=0, tiled=True)
        grad_out_w = lax.dot_general(
            normed_out, grad_full, CONTRACT_ROWS, preferred_element_type=jnp.float32
        )
        grad_normed_out = lax.dot_general(
            grad_full, out_weight[layer_index], CONTRACT_COLS, preferred_element_type=jnp.float32
        )
        grad_gnorm = jnp.sum(grad_normed_out * gated * inverse, axis=0)
        weighted = gnorm_gain[layer_index] * grad_normed_out
        inner_dot = lax.psum(jnp.sum(gated * weighted, axis=1), ("row", "col"))
        grad_gated = inverse * weighted - gated * inverse**3 * (inner_dot / inner_total)[:, None]
        (
            g_mixed,
            g_steps,
            g_side,
            g_conv_x,
            g_conv_x_bias,
            g_conv_bc,
            g_conv_bc_bias,
            g_dt_bias,
            g_a_log,
            g_skip,
        ) = pullback(grad_gated)
        mixed_rows, steps_rows = (
            lax.all_gather(g_mixed.astype(jnp.bfloat16), "col", axis=1, tiled=True),
            lax.all_gather(g_steps.astype(jnp.bfloat16), "col", axis=1, tiled=True),
        )
        grad_zx_w = lax.dot_general(
            gathered_cols, mixed_rows, CONTRACT_ROWS, preferred_element_type=jnp.float32
        )
        grad_dt_w = lax.dot_general(
            gathered_cols, steps_rows, CONTRACT_ROWS, preferred_element_type=jnp.float32
        )

        def back_rows(
            first_row,
            row_count,
            mixed_src=mixed_rows,
            steps_src=steps_rows,
            side_src=g_side,
            w_mixed=zx_weight[layer_index],
            w_steps=dt_weight[layer_index],
        ):
            main_part = lax.dot_general(
                mixed_src, w_mixed, CONTRACT_COLS, preferred_element_type=jnp.float32
            )
            main_part = main_part + lax.dot_general(
                steps_src, w_steps, CONTRACT_COLS, preferred_element_type=jnp.float32
            )
            return jnp.concatenate([main_part, side_src], axis=1)

        summed = lax.psum_scatter(
            back_rows(
                jnp.int32(0), lax.axis_size("row") * (mixed_rows.shape[0] // row_count_axis)
            ).astype(jnp.bfloat16),
            "row",
            scatter_dimension=0,
            tiled=True,
        ).astype(jnp.float32)
        all_cols = lax.all_gather(summed.astype(jnp.bfloat16), "col", axis=1, tiled=True).astype(
            summed.dtype
        )
        all_cols = all_cols.reshape(rows_here, col_count, col_width + state_width)
        grad_normed = all_cols[:, :, :col_width].reshape(rows_here, width)
        grad_side = jnp.sum(all_cols[:, :, col_width:], axis=1).astype(jnp.bfloat16)
        grad_normed = grad_normed + lax.dot_general(
            grad_side, bc_weight[layer_index], CONTRACT_COLS, preferred_element_type=jnp.float32
        )
        normed_local = lax.dynamic_slice_in_dim(normed, col_index * col_width, col_width, 1)
        bc_piece = lax.dot_general(
            normed_local, grad_side, CONTRACT_ROWS, preferred_element_type=jnp.float32
        )
        grad_bc_w = lax.dynamic_update_slice_in_dim(
            jnp.zeros((width, state_width), jnp.float32), bc_piece, col_index * col_width, 0
        )
        gain_terms = lax.dynamic_slice_in_dim(
            grad_normed * resid_in * scale, col_index * col_width, col_width, 1
        )
        grad_gain = lax.dynamic_update_slice_in_dim(
            jnp.zeros((width,), jnp.float32), jnp.sum(gain_terms, axis=0), col_index * col_width, 0
        )
        gain_dot = jnp.sum(resid_in * norm_gain[layer_index] * grad_normed, axis=1, keepdims=True)
        grad = (
            grad
            + scale * norm_gain[layer_index] * grad_normed
            - resid_in * scale**3 * gain_dot / width
        )
        head_tuple = (
            grad_zx_w,
            grad_dt_w,
            g_conv_x,
            g_conv_x_bias,
            g_dt_bias,
            g_a_log,
            g_skip,
            grad_gnorm,
            grad_out_w,
        )
        shared_tuple = (grad_gain, grad_bc_w, g_conv_bc, g_conv_bc_bias)
        heads_terms[layer_index] = head_tuple
        shared_terms[layer_index] = shared_tuple
    heads_stack = tuple(
        (jnp.stack([heads_terms[index][member] for index in range(layers)]) for member in range(9))
    )
    shared_stack = tuple(
        (jnp.stack([shared_terms[index][member] for index in range(layers)]) for member in range(4))
    )
    heads_stack = total_heads(heads_stack)
    shared_stack = total_shared(shared_stack)
    return (
        result_out,
        grad,
        shared_stack[0],
        heads_stack[0],
        heads_stack[1],
        shared_stack[1],
        heads_stack[2],
        heads_stack[3],
        shared_stack[2],
        shared_stack[3],
        heads_stack[4],
        heads_stack[5],
        heads_stack[6],
        heads_stack[7],
        heads_stack[8],
    )


def solution(mesh):
    placed = (
        P(("dp", "row"), None),
        P("dp", None),
        P(("dp", "row"), None),
        P(),
        P(None, "col", "row"),
        P(None, "col", "row"),
        P(),
        P(None, None, ("row", "col")),
        P(None, ("row", "col")),
        P(),
        P(),
        P(None, ("row", "col")),
        P(None, ("row", "col")),
        P(None, ("row", "col")),
        P(None, ("row", "col")),
        P(None, ("row", "col"), None),
    )
    return jax.shard_map(
        shards,
        mesh=mesh,
        in_specs=placed,
        out_specs=(
            P(("dp", "row"), None),
            P(("dp", "row"), None),
            P(),
            P(None, "col", "row"),
            P(None, "col", "row"),
            P(),
            P(None, None, ("row", "col")),
            P(None, ("row", "col")),
            P(),
            P(),
            P(None, ("row", "col")),
            P(None, ("row", "col")),
            P(None, ("row", "col")),
            P(None, ("row", "col")),
            P(None, ("row", "col"), None),
        ),
        check_vma=False,
    )
```

profile of v0, /device:TPU:0, one launch (start us, length us, event | category | flops | bytes accessed | tf_op | source)
XLA Modules:
  0.0 1166.4 jit_solution(9310738073706395560)
XLA Ops:
  12.0 11.5 all_gather.42
  23.6 2.7 fusion.148
  28.4 20.9 %all-reduce.74 = bf16[1024,8]{0,1:T(8,128)(2,1)S(1)} all-reduce(f32[1024,8]{0,1:T(8,128)S(1)} %fusion.316), channel_id=5, replica_groups=mesh['dp'=2,'row'=4,'col'=4] {'col'}, use_global_device_ids=true, to_apply=%region_2.0.clone | all-reduce | flops 8192 | bytes 49152
  50.6 2.4 reduce-window.26
  61.7 9.9 all_gather.43
  78.2 2.1 fusion.109
  82.4 22.0 %reduce-scatter.7.cloned.1.call-done = f32[1024,256]{1,0:T(8,128)} async-done(((f32[1024,1024]{1,0:T(8,128)}), f32[1024,256]{1,0:T(8,128)}) %reduce-scatter.7.cloned.1.call-update) | async-done | bytes 1048592 | tf_op jit(solution)/shard_map/reduce_scatter | solution.py:162
  104.3 2.3 convert_convert_fusion.1
  106.6 2.5 copy.258
  115.8 2.3 squeeze.43
  120.1 3.7 multiply_reduce_fusion.29
  123.8 41.3 %psum.119 = f32[1024]{0:T(1024)S(1)} all-reduce(f32[1024]{0:T(1024)S(1)} %bitcast.1228), channel_id=1, replica_groups=mesh['dp'=2,'row'=4,'col'=4] {'row','col'}, use_global_device_ids=true, to_apply=%region_6.8 | all-reduce | flops 1024 | bytes 8192 | tf_op jit(solution)/shard_map/psum | solution.py:181
  167.1 2.7 fusion.186
  169.9 93.9 %reduce-scatter.9.cloned.1.call-done = f32[64,1024]{1,0:T(8,128)} async-done(((f32[1024,1024]{1,0:T(8,128)}), f32[64,1024]{1,0:T(8,128)}) %reduce-scatter.9.cloned.1.call-update) | async-done | bytes 262160 | tf_op jit(solution)/shard_map/reduce_scatter | solution.py:189
  263.9 28.0 %all-gather.11.cloned.1.call-done = f32[256,1024]{1,0:T(8,128)} async-done(((f32[64,1024]{1,0:T(8,128)}), f32[256,1024]{1,0:T(8,128)}) %all-gather.11.cloned.1.call-update) | async-done | bytes 1048592 | tf_op jit(solution)/shard_map/all_gather | solution.py:195
  294.9 10.5 all_gather.45
  305.4 3.9 fusion.142
  312.0 19.0 %all-reduce.75 = bf16[1024,8]{0,1:T(8,128)(2,1)S(1)} all-reduce(f32[1024,8]{0,1:T(8,128)S(1)} %fusion.313), channel_id=8, replica_groups=mesh['dp'=2,'row'=4,'col'=4] {'col'}, use_global_device_ids=true, to_apply=%region_10.12.clone | all-reduce | flops 8192 | bytes 49152
  331.3 2.4 reduce-window.30
  335.1 13.8 %all_gather.46 = bf16[1024,256]{1,0:T(8,128)(2,1)S(1)} all-gather(bf16[256,256]{1,0:T(8,128)(2,1)S(1)} %convolution_convert_fusion.4), channel_id=1, replica_groups=mesh['dp'=2,'row'=4,'col'=4] {'row'}, dimensions={0}, use_global_device_ids=true | all-gather | bytes 655360 | tf_op jit(solution)/shard_map/all_gather | solution.py:153
  349.1 2.1 fusion.96
  353.0 3.1 fusion.386
  356.1 30.0 %reduce-scatter.11.cloned.1.call-done = f32[1024,256]{1,0:T(8,128)} async-done(((f32[1024,1024]{1,0:T(8,128)}), f32[1024,256]{1,0:T(8,128)}) %reduce-scatter.11.cloned.1.call-update) | async-done | bytes 1048592 | tf_op jit(solution)/shard_map/reduce_scatter | solution.py:162
  386.1 2.3 convert_convert_fusion
  388.4 2.6 copy.270
  407.9 3.6 multiply_reduce_fusion.28
  414.1 42.0 %psum.120 = f32[1024]{0:T(1024)} all-reduce(f32[1024]{0:T(1024)} %bitcast.1227), channel_id=1, replica_groups=mesh['dp'=2,'row'=4,'col'=4] {'row','col'}, use_global_device_ids=true, to_apply=%region_14.16 | all-reduce | flops 1024 | bytes 8192 | tf_op jit(solution)/shard_map/psum | solution.py:181
  457.4 4.5 multiply_reduce_fusion.14
  461.9 37.6 %psum.121 = f32[1024]{0:T(1024)} all-reduce(f32[1024]{0:T(1024)} %get-tuple-element.34), channel_id=1, replica_groups=mesh['dp'=2,'row'=4,'col'=4] {'row','col'}, use_global_device_ids=true, to_apply=%region_17.19 | all-reduce | flops 1024 | bytes 8192 | tf_op jit(solution)/shard_map/psum | solution.py:216
  500.2 3.2 fusion.124
  506.9 5.9 fusion.31
  518.7 2.5 convolution_bitcast_fusion.4
  529.0 3.7 fusion.36
  555.5 11.3 reduce-window.34
  579.2 14.0 %all-gather = bf16[1,1024,8]{1,0,2:T(2,128)(2,1)} all-gather(bf16[1,1024,2]{1,0,2:T(2,128)(2,1)S(1)} %copy.297), channel_id=2, replica_groups=mesh['dp'=2,'row'=4,'col'=4] {'col'}, dimensions={2}, use_global_device_ids=true | all-gather | bytes 20480 | tf_op jit(solution)/shard_map/all_gather | solution.py:232
  597.2 2.3 fusion.34
  604.8 2.3 fusion.140
  609.1 2.7 fusion.182
  611.9 22.6 %reduce-scatter.15.cloned.1.call-done = bf16[256,512]{1,0:T(8,128)(2,1)} async-done(((bf16[1024,512]{1,0:T(8,128)(2,1)}), bf16[256,512]{1,0:T(8,128)(2,1)}) %reduce-scatter.15.cloned.1.call-update) | async-done | bytes 262160 | tf_op jit(solution)/shard_map/reduce_scatter | solution.py:258
  634.6 115.4 %reduce-scatter.13.cloned.1.call-done = f32[64,1024]{1,0:T(8,128)} async-done(((f32[1024,1024]{1,0:T(8,128)}), f32[64,1024]{1,0:T(8,128)}) %reduce-scatter.13.cloned.1.call-update) | async-done | bytes 262160 | tf_op jit(solution)/shard_map/reduce_scatter | solution.py:189
  750.1 3.7 reshape.2426
  753.8 2.4 slice_reduce_fusion.1
  758.4 18.0 %all-gather.13.cloned.1.call-done = f32[256,1024]{1,0:T(8,128)} async-done(((f32[64,1024]{1,0:T(8,128)}), f32[256,1024]{1,0:T(8,128)}) %all-gather.13.cloned.1.call-update) | async-done | bytes 1048592 | tf_op jit(solution)/shard_map/all_gather | solution.py:195
  776.4 3.3 fusion.369
  783.6 30.7 %all-gather.21.cloned.1.call-done = bf16[1024,1024]{1,0:T(8,128)(2,1)} async-done(((bf16[256,1024]{1,0:T(8,128)(2,1)}), bf16[1024,1024]{1,0:T(8,128)(2,1)}) %all-gather.21.cloned.1.call-update) | async-done | bytes 2097168 | tf_op jit(solution)/shard_map/all_gather | solution.py:207
  814.3 4.4 multiply_reduce_fusion.15
  818.7 40.9 %psum.122 = f32[1024]{0:T(1024)S(1)} all-reduce(f32[1024]{0:T(1024)S(1)} %get-tuple-element.32), channel_id=1, replica_groups=mesh['dp'=2,'row'=4,'col'=4] {'row','col'}, use_global_device_ids=true, to_apply=%region_35.37 | all-reduce | flops 1024 | bytes 8192 | tf_op jit(solution)/shard_map/psum | solution.py:216
  859.7 3.2 fusion.125
  866.4 5.5 fusion.33
  880.9 3.7 fusion.45
  907.3 11.3 reduce-window.36
  930.9 14.0 %all-gather.1 = bf16[1,1024,8]{1,0,2:T(2,128)(2,1)} all-gather(bf16[1,1024,2]{1,0,2:T(2,128)(2,1)S(1)} %copy.319), channel_id=3, replica_groups=mesh['dp'=2,'row'=4,'col'=4] {'col'}, dimensions={2}, use_global_device_ids=true | all-gather | bytes 20480 | tf_op jit(solution)/shard_map/all_gather | solution.py:232
  948.5 2.3 fusion.35
  955.8 2.4 fusion.146
  962.6 2.2 fusion.55
  966.7 18.4 %reduce-scatter.17.cloned.1.call-done = bf16[256,512]{1,0:T(8,128)(2,1)} async-done(((bf16[1024,512]{1,0:T(8,128)(2,1)}), bf16[256,512]{1,0:T(8,128)(2,1)}) %reduce-scatter.17.cloned.1.call-update) | async-done | bytes 262160 | tf_op jit(solution)/shard_map/reduce_scatter | solution.py:258
  995.0 3.6 all-reduce.77
  1002.7 10.6 all-gather.25.cloned.1.call-done
  1013.3 3.7 reshape.2428
  1017.0 2.2 slice_reduce_fusion
  1022.6 2.8 convert_element_type.209
  1028.6 40.7 %all-reduce.76 = (f32[2,1024]{1,0:T(2,128)}, f32[2,4,256]{2,1,0:T(4,128)}, f32[2,256]{1,0:T(2,128)}) all-reduce(f32[2,1024]{1,0:T(2,128)S(1)} %pad_maximum_fusion.5, f32[2,4,256]{2,1,0:T(4,128)S(1)} %pad_maximum_fusion.7, f32[2,256]{1,0:T(2,128)S(1)} %pad_maximum_fusion.9), channel_id=1, replica_groups=mesh['dp'=2,'row'=4,'col'=4] {'dp','row','col'}, use_global_device_ids=true, to_apply=%region_54.56 | all-reduce | flops 4608 | bytes 36864 | tf_op jit(solution)/shard_map/psum | solution.py:112
  1070.7 85.3 %all-reduce.82.cloned.1.call-done = f32[2,1024,256]{2,1,0:T(8,128)} async-done(((f32[2,1024,256]{2,1,0:T(8,128)}), f32[2,1024,256]{2,1,0:T(8,128)}) %all-reduce.82.cloned.1.call-update) | async-done | bytes 2097168 | tf_op jit(solution)/shard_map/psum | solution.py:112
  1156.0 3.0 copy.438
  (787 shorter events, 214.3 us)
Async XLA Ops:
  8.0 96.3 %reduce-scatter.7.cloned.1.call-start = ((), (), s32[]{:S(2)}) async-start(), calls=%async_computation.6 | async-start | bytes 5242880 | tf_op jit(solution)/shard_map/reduce_scatter | solution.py:162
  8.9 285.1 %copy-start.111 = (f32[1,1024]{1,0:T(1,128)}, f32[1,1024]{1,0:T(1,128)S(1)}, u32[]{:S(2)}) copy-start(f32[1,1024]{1,0:T(1,128)S(1)} %get-tuple-element.187) | copy-start | bytes 12292
  12.0 49.4 %copy-start.54 = (bf16[256,1024]{1,0:T(8,128)(2,1)}, bf16[256,1024]{1,0:T(8,128)(2,1)S(1)}, u32[]{:S(2)}) copy-start(bf16[256,1024]{1,0:T(8,128)(2,1)S(1)} %fusion.68) | copy-start | bytes 1572868
  26.3 27.8 %copy-start.100 = (s32[1,1024]{1,0:T(1,128)S(1)}, s32[1,1024]{1,0:T(1,128)}, u32[]{:S(2)}) copy-start(s32[1,1024]{1,0:T(1,128)} %param.18) | copy-start | bytes 12292
  26.3 32.1 %copy-start.218 = (f32[2,128]{1,0:T(2,128)S(1)}, f32[2,128]{1,0:T(2,128)}, u32[]{:S(2)}) copy-start(f32[2,128]{1,0:T(2,128)} %param.31) | copy-start | bytes 3076
  26.3 35.1 %copy-start.68 = (bf16[2,1024,256]{2,1,0:T(8,128)(2,1)S(1)}, bf16[2,1024,256]{2,1,0:T(8,128)(2,1)}, u32[]{:S(2)}) copy-start(bf16[2,1024,256]{2,1,0:T(8,128)(2,1)} %param.23) | copy-start | bytes 3145732
  26.3 45.6 %copy-start.220 = (f32[2,128]{1,0:T(2,128)S(1)}, f32[2,128]{1,0:T(2,128)}, u32[]{:S(2)}) copy-start(f32[2,128]{1,0:T(2,128)} %param.25) | copy-start | bytes 3076
  26.3 46.1 %copy-start.221 = (f32[2,2]{1,0:T(2,128)S(1)}, f32[2,2]{1,0:T(2,128)}, u32[]{:S(2)}) copy-start(f32[2,2]{1,0:T(2,128)} %param.30) | copy-start | bytes 52
  26.4 46.7 %copy-start.214 = (f32[2,256]{1,0:T(2,128)S(1)}, f32[2,256]{1,0:T(2,128)}, u32[]{:S(2)}) copy-start(f32[2,256]{1,0:T(2,128)} %param.27) | copy-start | bytes 6148
  26.4 47.2 %copy-start.201 = (f32[2,4,128]{2,1,0:T(4,128)S(1)}, f32[2,4,128]{2,1,0:T(4,128)}, u32[]{:S(2)}) copy-start(f32[2,4,128]{2,1,0:T(4,128)} %param.24) | copy-start | bytes 12292
  26.4 49.9 %copy-start.166 = (f32[2,4,256]{2,1,0:T(4,128)S(1)}, f32[2,4,256]{2,1,0:T(4,128)}, u32[]{:S(2)}) copy-start(f32[2,4,256]{2,1,0:T(4,128)} %param.26) | copy-start | bytes 24580
  26.4 237.4 %reduce-scatter.9.cloned.1.call-start = ((), (), s32[]{:S(2)}) async-start(), calls=%async_computation.7 | async-start | bytes 4456448 | tf_op jit(solution)/shard_map/reduce_scatter | solution.py:189
  50.5 69.5 %copy-start.95 = (f32[1,1024,2]{1,2,0:T(2,128)}, f32[1,1024,2]{1,2,0:T(2,128)S(1)}, u32[]{:S(2)}) copy-start(f32[1,1024,2]{1,2,0:T(2,128)S(1)} %compare_select_fusion.5) | copy-start | bytes 24580
  71.8 47.0 %copy-start.159 = (f32[2]{0:T(128)}, f32[2]{0:T(128)S(1)}, u32[]{:S(2)}) copy-start(f32[2]{0:T(128)S(1)} %get-tuple-element.56) | copy-start | bytes 28
  71.8 47.0 %copy-start.184 = (f32[2]{0:T(128)}, f32[2]{0:T(128)S(1)}, u32[]{:S(2)}) copy-start(f32[2]{0:T(128)S(1)} %get-tuple-element.55) | copy-start | bytes 28
  74.2 37.1 %copy-start.167 = (f32[128]{0:T(128)}, f32[128]{0:T(128)S(1)}, u32[]{:S(2)}) copy-start(f32[128]{0:T(128)S(1)} %get-tuple-element.201) | copy-start | bytes 1540
  74.2 37.1 %copy-start.169 = (f32[128]{0:T(128)}, f32[128]{0:T(128)S(1)}, u32[]{:S(2)}) copy-start(f32[128]{0:T(128)S(1)} %get-tuple-element.198) | copy-start | bytes 1540
  74.2 37.1 %copy-start.171 = (f32[128]{0:T(128)}, f32[128]{0:T(128)S(1)}, u32[]{:S(2)}) copy-start(f32[128]{0:T(128)S(1)} %get-tuple-element.199) | copy-start | bytes 1540
  74.2 37.1 %copy-start.173 = (f32[128]{0:T(128)}, f32[128]{0:T(128)S(1)}, u32[]{:S(2)}) copy-start(f32[128]{0:T(128)S(1)} %get-tuple-element.200) | copy-start | bytes 1540
  76.2 276.1 %copy-start.99 = (f32[4,256]{1,0:T(4,128)}, f32[4,256]{1,0:T(4,128)S(1)}, u32[]{:S(2)}) copy-start(f32[4,256]{1,0:T(4,128)S(1)} %compare_convert_fusion.6) | copy-start | bytes 12292
  76.3 43.6 %copy-start.122 = (f32[256,2]{0,1:T(2,128)}, f32[256,2]{0,1:T(2,128)S(1)}, u32[]{:S(2)}) copy-start(f32[256,2]{0,1:T(2,128)S(1)} %get-tuple-element.189) | copy-start | bytes 6148
  76.3 43.7 %copy-start.124 = (f32[256,2]{0,1:T(2,128)}, f32[256,2]{0,1:T(2,128)S(1)}, u32[]{:S(2)}) copy-start(f32[256,2]{0,1:T(2,128)S(1)} %get-tuple-element.190) | copy-start | bytes 6148
  76.3 43.7 %copy-start.126 = (f32[256,2]{0,1:T(2,128)}, f32[256,2]{0,1:T(2,128)S(1)}, u32[]{:S(2)}) copy-start(f32[256,2]{0,1:T(2,128)S(1)} %get-tuple-element.191) | copy-start | bytes 6148
  77.0 316.1 %copy-start.83 = (f32[1,1024]{1,0:T(1,128)}, f32[1,1024]{1,0:T(1,128)S(1)}, u32[]{:S(2)}) copy-start(f32[1,1024]{1,0:T(1,128)S(1)} %get-tuple-element.207) | copy-start | bytes 12292
  77.0 316.1 %copy-start.86 = (f32[1,1024]{1,0:T(1,128)}, f32[1,1024]{1,0:T(1,128)S(1)}, u32[]{:S(2)}) copy-start(f32[1,1024]{1,0:T(1,128)S(1)} %get-tuple-element.208) | copy-start | bytes 12292
  77.0 316.1 %copy-start.89 = (f32[1,1024]{1,0:T(1,128)}, f32[1,1024]{1,0:T(1,128)S(1)}, u32[]{:S(2)}) copy-start(f32[1,1024]{1,0:T(1,128)S(1)} %get-tuple-element.209) | copy-start | bytes 12292
  77.1 41.0 %copy-start.105 = (f32[4,256,2]{1,2,0:T(2,128)}, f32[4,256,2]{1,2,0:T(2,128)S(1)}, u32[]{:S(2)}) copy-start(f32[4,256,2]{1,2,0:T(2,128)S(1)} %multiply_bitcast_fusion.7) | copy-start | bytes 24580
  80.4 37.7 %copy-start.4 = (f32[1,1024,128]{2,1,0:T(8,128)}, f32[1,1024,128]{2,1,0:T(8,128)S(1)}, u32[]{:S(2)}) copy-start(f32[1,1024,128]{2,1,0:T(8,128)S(1)} %get-tuple-element.150) | copy-start | bytes 1572868
  80.4 39.2 %copy-start.13 = (f32[1,1024,128]{2,1,0:T(8,128)}, f32[1,1024,128]{2,1,0:T(8,128)S(1)}, u32[]{:S(2)}) copy-start(f32[1,1024,128]{2,1,0:T(8,128)S(1)} %get-tuple-element.151) | copy-start | bytes 1572868
  120.1 45.7 %copy-start.217 = (f32[2,64]{1,0:T(2,128)S(1)}, f32[2,64]{1,0:T(2,128)}, u32[]{:S(2)}) copy-start(f32[2,64]{1,0:T(2,128)} %mul.2202) | copy-start | bytes 1540
  120.1 47.0 %copy-start.79 = (bf16[2,128,1024]{2,1,0:T(8,128)(2,1)S(1)}, bf16[2,128,1024]{2,1,0:T(8,128)(2,1)}, u32[]{:S(2)}) copy-start(bf16[2,128,1024]{2,1,0:T(8,128)(2,1)} %param.32) | copy-start | bytes 1572868
  169.9 122.0 %copy-start.2 = (bf16[256,1024]{1,0:T(8,128)(2,1)S(1)}, bf16[256,1024]{1,0:T(8,128)(2,1)}, u32[]{:S(2)}) copy-start(bf16[256,1024]{1,0:T(8,128)(2,1)} %param.17) | copy-start | bytes 1572868
  169.9 122.0 %all-gather.11.cloned.1.call-start = ((), (), s32[]{:S(2)}) async-start(), calls=%async_computation.8 | async-start | bytes 1310720 | tf_op jit(solution)/shard_map/all_gather | solution.py:195
  263.8 122.2 %reduce-scatter.11.cloned.1.call-start = ((), (), s32[]{:S(2)}) async-start(), calls=%async_computation.9 | async-start | bytes 5242880 | tf_op jit(solution)/shard_map/reduce_scatter | solution.py:162
  309.4 25.1 %copy-start.134 = (f32[1,1,256]{2,1,0:T(1,128)S(1)}, f32[1,1,256]{2,1,0:T(1,128)}, u32[]{:S(2)}) copy-start(f32[1,1,256]{2,1,0:T(1,128)} %copy-done.133) | copy-start | bytes 3076
  309.4 25.1 %copy-start.136 = (f32[1,1,256]{2,1,0:T(1,128)S(1)}, f32[1,1,256]{2,1,0:T(1,128)}, u32[]{:S(2)}) copy-start(f32[1,1,256]{2,1,0:T(1,128)} %copy-done.135) | copy-start | bytes 3076
  309.4 147.9 %all-gather.15.cloned.1.call-start = ((), (), s32[]{:S(2)}) async-start(), calls=%async_computation.12 | async-start | bytes 2621440 | tf_op jit(solution)/shard_map/all_gather | solution.py:207
  310.0 39.0 %copy-start.149 = (f32[1,1,256]{2,1,0:T(1,128)S(1)}, f32[1,1,256]{2,1,0:T(1,128)}, u32[]{:S(2)}) copy-start(f32[1,1,256]{2,1,0:T(1,128)} %get-tuple-element.185) | copy-start | bytes 3076
  310.0 39.0 %copy-start.151 = (f32[1,1,256]{2,1,0:T(1,128)S(1)}, f32[1,1,256]{2,1,0:T(1,128)}, u32[]{:S(2)}) copy-start(f32[1,1,256]{2,1,0:T(1,128)} %get-tuple-element.186) | copy-start | bytes 3076
  310.0 39.0 %copy-start.153 = (f32[1,1,256]{2,1,0:T(1,128)S(1)}, f32[1,1,256]{2,1,0:T(1,128)}, u32[]{:S(2)}) copy-start(f32[1,1,256]{2,1,0:T(1,128)} %get-tuple-element.180) | copy-start | bytes 3076
  310.0 39.0 %copy-start.157 = (f32[1,1,256]{2,1,0:T(1,128)S(1)}, f32[1,1,256]{2,1,0:T(1,128)}, u32[]{:S(2)}) copy-start(f32[1,1,256]{2,1,0:T(1,128)} %get-tuple-element.179) | copy-start | bytes 3076
  310.1 39.0 %copy-start.193 = (f32[1,256]{1,0:T(1,128)S(1)}, f32[1,256]{1,0:T(1,128)}, u32[]{:S(2)}) copy-start(f32[1,256]{1,0:T(1,128)} %get-tuple-element.210) | copy-start | bytes 3076
  310.1 294.4 %all-gather.17.cloned.1.call-start = ((), (), s32[]{:S(2)}) async-start(), calls=%async_computation.13 | async-start | bytes 2621440 | tf_op jit(solution)/shard_map/all_gather | solution.py:231
  334.5 68.6 %copy-start.161 = (f32[2]{0:T(128)}, f32[2]{0:T(128)S(1)}, u32[]{:S(2)}) copy-start(f32[2]{0:T(128)S(1)} %get-tuple-element.54) | copy-start | bytes 28
  334.5 68.6 %copy-start.186 = (f32[2]{0:T(128)}, f32[2]{0:T(128)S(1)}, u32[]{:S(2)}) copy-start(f32[2]{0:T(128)S(1)} %get-tuple-element.53) | copy-start | bytes 28
  352.1 36.3 %copy-start.6 = (f32[1,1024,128]{2,1,0:T(8,128)}, f32[1,1024,128]{2,1,0:T(8,128)S(1)}, u32[]{:S(2)}) copy-start(f32[1,1024,128]{2,1,0:T(8,128)S(1)} %get-tuple-element.146) | copy-start | bytes 1572868
  352.3 36.1 %copy-start.132 = (f32[4,2]{1,0:T(4,128)}, f32[4,2]{1,0:T(4,128)S(1)}, u32[]{:S(2)}) copy-start(f32[4,2]{1,0:T(4,128)S(1)} %copy.275) | copy-start | bytes 100
  352.4 48.6 %copy-start.107 = (f32[4,256,2]{1,2,0:T(2,128)}, f32[4,256,2]{1,2,0:T(2,128)S(1)}, u32[]{:S(2)}) copy-start(f32[4,256,2]{1,2,0:T(2,128)S(1)} %multiply_bitcast_fusion.6) | copy-start | bytes 24580
  540.9 52.3 %copy-start.78 = (f32[1,1,2,128,64]{3,4,2,1,0:T(8,128)S(1)}, f32[1,1,2,128,64]{3,4,2,1,0:T(8,128)}, u32[]{:S(2)}) copy-start(f32[1,1,2,128,64]{3,4,2,1,0:T(8,128)} %copy-done.77) | copy-start | bytes 196612
  541.7 52.8 %copy-start.76 = (f32[1,1,2,128,64]{3,4,2,1,0:T(8,128)S(1)}, f32[1,1,2,128,64]{3,4,2,1,0:T(8,128)}, u32[]{:S(2)}) copy-start(f32[1,1,2,128,64]{3,4,2,1,0:T(8,128)} %copy-done.75) | copy-start | bytes 196612
  541.8 55.4 %copy-start.8 = (f32[1,1024,128]{2,1,0:T(8,128)S(1)}, f32[1,1024,128]{2,1,0:T(8,128)}, u32[]{:S(2)}) copy-start(f32[1,1024,128]{2,1,0:T(8,128)} %copy-done.6) | copy-start | bytes 1572868
  542.6 91.9 %reduce-scatter.15.cloned.1.call-start = ((), (), s32[]{:S(2)}) async-start(), calls=%async_computation.14 | async-start | bytes 1310720 | tf_op jit(solution)/shard_map/reduce_scatter | solution.py:258
  608.6 141.4 %reduce-scatter.13.cloned.1.call-start = ((), (), s32[]{:S(2)}) async-start(), calls=%async_computation.10 | async-start | bytes 4456448 | tf_op jit(solution)/shard_map/reduce_scatter | solution.py:189
  611.9 138.2 %all-gather.19.cloned.1.call-start = ((), (), s32[]{:S(2)}) async-start(), calls=%async_computation.15 | async-start | bytes 1310720 | tf_op jit(solution)/shard_map/all_gather | solution.py:266
  634.5 141.9 %all-gather.13.cloned.1.call-start = ((), (), s32[]{:S(2)}) async-start(), calls=%async_computation.11 | async-start | bytes 1310720 | tf_op jit(solution)/shard_map/all_gather | solution.py:195
  750.0 64.3 %all-gather.21.cloned.1.call-start = ((), (), s32[]{:S(2)}) async-start(), calls=%async_computation.16 | async-start | bytes 2621440 | tf_op jit(solution)/shard_map/all_gather | solution.py:207
  779.7 176.1 %all-gather.23.cloned.1.call-start = ((), (), s32[]{:S(2)}) async-start(), calls=%async_computation.17 | async-start | bytes 2621440 | tf_op jit(solution)/shard_map/all_gather | solution.py:231
  893.7 51.3 %copy-start.24 = (f32[1,4,256,2,64]{2,4,3,1,0:T(8,128)S(1)}, f32[1,4,256,2,64]{2,4,3,1,0:T(8,128)}, u32[]{:S(2)}) copy-start(f32[1,4,256,2,64]{2,4,3,1,0:T(8,128)} %copy-done.23) | copy-start | bytes 1572868
  894.6 90.5 %reduce-scatter.17.cloned.1.call-start = ((), (), s32[]{:S(2)}) async-start(), calls=%async_computation.18 | async-start | bytes 1310720 | tf_op jit(solution)/shard_map/reduce_scatter | solution.py:258
  959.9 53.4 %all-gather.25.cloned.1.call-start = ((), (), s32[]{:S(2)}) async-start(), calls=%async_computation.19 | async-start | bytes 1310720 | tf_op jit(solution)/shard_map/all_gather | solution.py:266
  985.2 37.4 %all-reduce.84.cloned.1.call-start = ((), (), s32[]{:S(2)}) async-start(), calls=%async_computation.21 | async-start | bytes 3145728 | tf_op jit(solution)/shard_map/psum | solution.py:108
  994.7 161.4 %all-reduce.82.cloned.1.call-start = ((), (), s32[]{:S(2)}) async-start(), calls=%async_computation.20 | async-start | bytes 4194304 | tf_op jit(solution)/shard_map/psum | solution.py:112
  1026.8 42.6 %copy-start.37 = (f32[256,1024]{1,0:T(8,128)S(1)}, f32[256,1024]{1,0:T(8,128)}, u32[]{:S(2)}) copy-start(f32[256,1024]{1,0:T(8,128)} %get-tuple-element.111) | copy-start | bytes 3145732
  1026.8 42.6 %copy-start.192 = (f32[256]{0:T(256)S(1)}, f32[256]{0:T(256)}, u32[]{:S(2)}) copy-start(f32[256]{0:T(256)} %get-tuple-element.214) | copy-start | bytes 3076
  (187 other events, 996.1 us)
Sparse Core Ops, SparseCore 0:
  26.5 77.8 reduce-scatter.6
  170.0 93.7 reduce-scatter.8
  265.4 26.4 all-gather.10
  309.5 76.5 reduce-scatter.10
  542.8 43.7 all-gather.16
  634.7 45.0 all-gather.18
  750.2 26.2 all-gather.12
  894.7 43.2 all-gather.22
  985.3 27.9 all-gather.24
Sparse Core Ops, SparseCore 1:
  311.8 36.3 all-gather.14
  608.7 25.8 reduce-scatter.14
  636.7 113.3 reduce-scatter.12
  779.8 34.4 all-gather.20
  960.0 25.1 reduce-scatter.16
  994.7 20.0 all-reduce.83
  1022.0 134.0 all-reduce.81
where the time goes:
time: 1180 us; the launch traced here: 1170 us
  waiting for transfers between devices  476 us (40%)
  blocking collectives  320 us (27%)
  other arithmetic  141 us (12%)
  matrix products  104 us (9%)
  local copies, waits for them, and re-layouts  102 us (9%)
  between operations  21.9 us (2%)
    reduce_scatter x2, waiting for transfers between devices, shards(): lax.psum_scatter(project(jnp.int32(0), lax.axis_size(('row', 'col')) * ke...  209 us
    psum x1, waiting for transfers between devices, total_shared(): return lax.psum(terms, ('dp', 'row', 'col'))  85.3 us
    psum x2, blocking collectives, shards(): squares = lax.psum(jnp.sum(gated * gated, axis=1), ('row', 'col'))  83.3 us
    psum x2, blocking collectives, shards(): inner_dot = lax.psum(jnp.sum(gated * weighted, axis=1), ('row', 'col'))  78.5 us
    reduce_scatter x2, waiting for transfers between devices, shards(): lax.psum_scatter(part_mixed, 'col', scatter_dimension=1, tiled=True)  51.9 us
    all_gather x2, waiting for transfers between devices, shards(): branch = lax.all_gather(shared_rows, 'col', axis=0, tiled=True)  46 us
    reduce_scatter x2, waiting for transfers between devices, shards(): lax.psum_scatter(back_rows(jnp.int32(0), lax.axis_size('row') * (mixed_ro...  41 us
    psum x1, blocking collectives, total_shared(): return lax.psum(terms, ('dp', 'row', 'col'))  40.7 us
  transfers between devices with their start and end apart: 16, of which 11 were waited for; matrix products, arithmetic and copies ran while one was open for 17% of the time, Pallas kernels for 0%

commit v1 on v0

--- a/solution.py
+++ b/solution.py
@@ -204,7 +204,18 @@
             layer_index
         ]
         grad_low = grad.astype(jnp.bfloat16)
-        grad_full = lax.all_gather(grad_low, "row", axis=0, tiled=True)
+        piece_next, a_next = (jax.lax.psum(1, axis_name="row"), jax.lax.axis_index("row"))
+        grad_full, shaped = (grad_low, 1)
+        while shaped < piece_next:
+            z1 = jax.lax.ppermute(
+                grad_full,
+                axis_name="row",
+                perm=tuple(((k0, k0 ^ shaped) for k0 in range(piece_next))),
+            )
+            left_arr = jnp.concatenate([grad_full, z1], axis=0)
+            r_now = jnp.concatenate([z1, grad_full], axis=0)
+            grad_full = jnp.where(a_next & shaped == 0, left_arr, r_now)
+            shaped = 2 * shaped
         grad_out_w = lax.dot_general(
             normed_out, grad_full, CONTRACT_ROWS, preferred_element_type=jnp.float32
         )

time: 1180 us -> 1220 us (1.034)
  waiting for transfers between devices: 476 us -> 511 us
    ppermute x0 -> x4, waiting for transfers between devices: none -> 42.4 us  [shards(): jax.lax.ppermute(grad_full, axis_name='row', perm=tuple(((k0, k0 ^ shaped...]
    all_gather x2 -> x0, waiting for transfers between devices: 30.7 us -> none  [shards(): grad_full = lax.all_gather(grad_low, 'row', axis=0, tiled=True)]
    all_gather x2, waiting for transfers between devices: 10.6 us -> 39.5 us  [shards(): lax.all_gather(summed.astype(jnp.bfloat16), 'col', axis=1, tiled=True)]
    reduce_scatter x2, waiting for transfers between devices: 209 us -> 193 us  [shards(): lax.psum_scatter(project(jnp.int32(0), lax.axis_size(('row', 'col')) * ke...]
    psum x1, waiting for transfers between devices: 0.02 us -> 14 us  [total_heads(): lax.psum(shortened(terms), 'dp')]
  transfers between devices with their start and end apart: 16 -> 18, of which waited for: 11 -> 15; matrix products, arithmetic and copies ran while one was open for 17% -> 17% of each run, Pallas kernels for 0% -> 0%
where the time goes in v1:
time: 1220 us; the launch traced here: 1210 us
  waiting for transfers between devices  511 us (42%)
  blocking collectives  317 us (26%)
  other arithmetic  145 us (12%)
  matrix products  107 us (9%)
  local copies, waits for them, and re-layouts  100 us (8%)
  between operations  20.5 us (2%)
    reduce_scatter x2, waiting for transfers between devices, shards(): lax.psum_scatter(project(jnp.int32(0), lax.axis_size(('row', 'col')) * ke...  193 us
    psum x1, waiting for transfers between devices, total_shared(): return lax.psum(terms, ('dp', 'row', 'col'))  93.2 us
    psum x2, blocking collectives, shards(): squares = lax.psum(jnp.sum(gated * gated, axis=1), ('row', 'col'))  83.3 us
    psum x2, blocking collectives, shards(): inner_dot = lax.psum(jnp.sum(gated * weighted, axis=1), ('row', 'col'))  79.4 us
    all_gather x2, waiting for transfers between devices, shards(): branch = lax.all_gather(shared_rows, 'col', axis=0, tiled=True)  48.9 us
    ppermute x4, waiting for transfers between devices, shards(): jax.lax.ppermute(grad_full, axis_name='row', perm=tuple(((k0, k0 ^ shaped...  42.4 us
    reduce_scatter x2, waiting for transfers between devices, shards(): lax.psum_scatter(part_mixed, 'col', scatter_dimension=1, tiled=True)  41.6 us
    psum x1, blocking collectives, total_shared(): return lax.psum(terms, ('dp', 'row', 'col'))  41.4 us
  transfers between devices with their start and end apart: 18, of which 15 were waited for; matrix products, arithmetic and copies ran while one was open for 17% of the time, Pallas kernels for 0%

profile of v1, /device:TPU:0, one launch (start us, length us, event | category | flops | bytes accessed | tf_op | source)
XLA Modules:
  0.0 1208.5 jit_solution(473634511909515958)
XLA Ops:
  11.1 11.5 all_gather.36
  22.7 2.7 fusion.148
  27.5 20.9 %all-reduce.74 = bf16[1024,8]{0,1:T(8,128)(2,1)S(1)} all-reduce(f32[1024,8]{0,1:T(8,128)S(1)} %fusion.316), channel_id=5, replica_groups=mesh['dp'=2,'row'=4,'col'=4] {'col'}, use_global_device_ids=true, to_apply=%region_2.0.clone | all-reduce | flops 8192 | bytes 49152
  49.7 2.4 reduce-window.26
  60.7 9.9 all_gather.37
  81.4 22.0 %reduce-scatter.7.cloned.1.call-done = f32[1024,256]{1,0:T(8,128)} async-done(((f32[1024,1024]{1,0:T(8,128)}), f32[1024,256]{1,0:T(8,128)}) %reduce-scatter.7.cloned.1.call-update) | async-done | bytes 1048592 | tf_op jit(solution)/shard_map/reduce_scatter | solution.py:162
  105.7 2.5 copy.258
  119.2 3.7 multiply_reduce_fusion.29
  122.9 41.3 %psum.119 = f32[1024]{0:T(1024)S(1)} all-reduce(f32[1024]{0:T(1024)S(1)} %bitcast.1224), channel_id=1, replica_groups=mesh['dp'=2,'row'=4,'col'=4] {'row','col'}, use_global_device_ids=true, to_apply=%region_6.8 | all-reduce | flops 1024 | bytes 8192 | tf_op jit(solution)/shard_map/psum | solution.py:181
  166.3 2.7 fusion.186
  169.1 93.7 %reduce-scatter.9.cloned.1.call-done = f32[64,1024]{1,0:T(8,128)} async-done(((f32[1024,1024]{1,0:T(8,128)}), f32[64,1024]{1,0:T(8,128)}) %reduce-scatter.9.cloned.1.call-update) | async-done | bytes 262160 | tf_op jit(solution)/shard_map/reduce_scatter | solution.py:189
  262.9 28.2 %all-gather.9.cloned.1.call-done = f32[256,1024]{1,0:T(8,128)} async-done(((f32[64,1024]{1,0:T(8,128)}), f32[256,1024]{1,0:T(8,128)}) %all-gather.9.cloned.1.call-update) | async-done | bytes 1048592 | tf_op jit(solution)/shard_map/all_gather | solution.py:195
  294.1 10.5 all_gather.39
  304.6 3.9 fusion.142
  311.4 9.8 collective-permute-done
  321.2 2.7 maximum_select_fusion.2
  325.2 19.9 %all-reduce.75 = bf16[1024,8]{0,1:T(8,128)(2,1)S(1)} all-reduce(f32[1024,8]{0,1:T(8,128)S(1)} %fusion.313), channel_id=8, replica_groups=mesh['dp'=2,'row'=4,'col'=4] {'col'}, use_global_device_ids=true, to_apply=%region_10.12.clone | all-reduce | flops 8192 | bytes 49152
  345.4 2.4 reduce-window.30
  350.6 8.9 all_gather.40
  365.9 19.5 %reduce-scatter.11.cloned.1.call-done = f32[1024,256]{1,0:T(8,128)} async-done(((f32[1024,1024]{1,0:T(8,128)}), f32[1024,256]{1,0:T(8,128)}) %reduce-scatter.11.cloned.1.call-update) | async-done | bytes 1048592 | tf_op jit(solution)/shard_map/reduce_scatter | solution.py:162
  385.4 2.3 convert_convert_fusion
  387.7 2.5 copy.270
  406.5 3.6 multiply_reduce_fusion.28
  412.7 42.0 %psum.120 = f32[1024]{0:T(1024)} all-reduce(f32[1024]{0:T(1024)} %bitcast.1223), channel_id=1, replica_groups=mesh['dp'=2,'row'=4,'col'=4] {'row','col'}, use_global_device_ids=true, to_apply=%region_14.16 | all-reduce | flops 1024 | bytes 8192 | tf_op jit(solution)/shard_map/psum | solution.py:181
  456.0 5.3 multiply_reduce_fusion.14
  461.3 37.6 %psum.121 = f32[1024]{0:T(1024)} all-reduce(f32[1024]{0:T(1024)} %get-tuple-element.34), channel_id=1, replica_groups=mesh['dp'=2,'row'=4,'col'=4] {'row','col'}, use_global_device_ids=true, to_apply=%region_17.19 | all-reduce | flops 1024 | bytes 8192 | tf_op jit(solution)/shard_map/psum | solution.py:227
  499.6 3.1 fusion.124
  506.2 5.9 fusion.31
  518.0 2.5 convolution_bitcast_fusion.4
  528.3 3.7 fusion.36
  554.6 11.2 reduce-window.34
  578.2 14.1 %all-gather = bf16[1,1024,8]{1,0,2:T(2,128)(2,1)} all-gather(bf16[1,1024,2]{1,0,2:T(2,128)(2,1)S(1)} %copy.297), channel_id=2, replica_groups=mesh['dp'=2,'row'=4,'col'=4] {'col'}, dimensions={2}, use_global_device_ids=true | all-gather | bytes 20480 | tf_op jit(solution)/shard_map/all_gather | solution.py:243
  603.8 2.4 fusion.140
  608.2 2.7 fusion.183
  611.0 22.6 %reduce-scatter.15.cloned.1.call-done = bf16[256,512]{1,0:T(8,128)(2,1)} async-done(((bf16[1024,512]{1,0:T(8,128)(2,1)}), bf16[256,512]{1,0:T(8,128)(2,1)}) %reduce-scatter.15.cloned.1.call-update) | async-done | bytes 262160 | tf_op jit(solution)/shard_map/reduce_scatter | solution.py:269
  633.6 99.6 %reduce-scatter.13.cloned.1.call-done = f32[64,1024]{1,0:T(8,128)} async-done(((f32[1024,1024]{1,0:T(8,128)}), f32[64,1024]{1,0:T(8,128)}) %reduce-scatter.13.cloned.1.call-update) | async-done | bytes 262160 | tf_op jit(solution)/shard_map/reduce_scatter | solution.py:189
  733.3 28.2 %all-gather.15.cloned.1.call-done = bf16[256,2048]{1,0:T(8,128)(2,1)} async-done(((bf16[256,512]{1,0:T(8,128)(2,1)}), bf16[256,2048]{1,0:T(8,128)(2,1)}) %all-gather.15.cloned.1.call-update) | async-done | bytes 1048592 | tf_op jit(solution)/shard_map/all_gather | solution.py:277
  761.4 3.7 reshape.2426
  765.1 2.4 slice_reduce_fusion.1
  769.7 20.8 %all-gather.11.cloned.1.call-done = f32[256,1024]{1,0:T(8,128)} async-done(((f32[64,1024]{1,0:T(8,128)}), f32[256,1024]{1,0:T(8,128)}) %all-gather.11.cloned.1.call-update) | async-done | bytes 1048592 | tf_op jit(solution)/shard_map/all_gather | solution.py:195
  790.4 3.2 fusion.373
  795.1 11.7 collective-permute-done.2
  811.2 20.9 %collective-permute-done.3 = bf16[512,1024]{1,0:T(8,128)(2,1)} collective-permute-done((bf16[512,1024]{1,0:T(8,128)(2,1)}, bf16[512,1024]{1,0:T(8,128)(2,1)}, u32[]{:S(2)}, u32[]{:S(2)}) %collective-permute-start.3) | collective-permute-done | bytes 1048608 | tf_op jit(solution)/shard_map/ppermute | solution.py:210
  832.1 5.1 multiply_reduce_fusion.15
  837.2 41.8 %psum.122 = f32[1024]{0:T(1024)S(1)} all-reduce(f32[1024]{0:T(1024)S(1)} %get-tuple-element.32), channel_id=1, replica_groups=mesh['dp'=2,'row'=4,'col'=4] {'row','col'}, use_global_device_ids=true, to_apply=%region_35.37 | all-reduce | flops 1024 | bytes 8192 | tf_op jit(solution)/shard_map/psum | solution.py:227
  879.0 3.2 fusion.125
  885.8 5.5 fusion.33
  900.4 3.7 fusion.45
  926.8 11.3 reduce-window.36
  950.4 13.9 %all-gather.1 = bf16[1,1024,8]{1,0,2:T(2,128)(2,1)} all-gather(bf16[1,1024,2]{1,0,2:T(2,128)(2,1)S(1)} %copy.319), channel_id=3, replica_groups=mesh['dp'=2,'row'=4,'col'=4] {'col'}, dimensions={2}, use_global_device_ids=true | all-gather | bytes 20480 | tf_op jit(solution)/shard_map/all_gather | solution.py:243
  967.9 2.3 fusion.35
  975.3 2.4 fusion.146
  982.0 3.1 fusion.55
  988.0 15.9 %reduce-scatter.17.cloned.1.call-done = bf16[256,512]{1,0:T(8,128)(2,1)} async-done(((bf16[1024,512]{1,0:T(8,128)(2,1)}), bf16[256,512]{1,0:T(8,128)(2,1)}) %reduce-scatter.17.cloned.1.call-update) | async-done | bytes 262160 | tf_op jit(solution)/shard_map/reduce_scatter | solution.py:269
  1008.1 3.1 fusion.54
  1014.4 3.6 all-reduce.77
  1022.1 11.3 all-gather.19.cloned.1.call-done
  1033.4 3.7 reshape.2428
  1037.1 2.3 slice_reduce_fusion
  1042.7 14.0 %all-reduce.84.cloned.1.call-done = (bf16[2,256,1024]{2,1,0:T(8,128)(2,1)}, bf16[2,128,1024]{2,1,0:T(8,128)(2,1)}) async-done(((bf16[2,256,1024]{2,1,0:T(8,128)(2,1)}, bf16[2,128,1024]{2,1,0:T(8,128)(2,1)}), (bf16[2,256,1024]{2,1,0:T(8,128)(2,1)}, bf16[2,128,1024]{2,1,0:T(8,128)(2,1)})) %all-reduce.84.cloned.1.call-update) | async-done | bytes 1572880 | tf_op jit(solution)/shard_map/psum | solution.py:108
  1056.7 2.8 convert_element_type.209
  1062.7 41.4 %all-reduce.76 = (f32[2,1024]{1,0:T(2,128)}, f32[2,4,256]{2,1,0:T(4,128)}, f32[2,256]{1,0:T(2,128)}) all-reduce(f32[2,1024]{1,0:T(2,128)S(1)} %pad_maximum_fusion.5, f32[2,4,256]{2,1,0:T(4,128)S(1)} %pad_maximum_fusion.7, f32[2,256]{1,0:T(2,128)S(1)} %pad_maximum_fusion.9), channel_id=1, replica_groups=mesh['dp'=2,'row'=4,'col'=4] {'dp','row','col'}, use_global_device_ids=true, to_apply=%region_54.56 | all-reduce | flops 4608 | bytes 36864 | tf_op jit(solution)/shard_map/psum | solution.py:112
  1105.5 93.2 %all-reduce.82.cloned.1.call-done = f32[2,1024,256]{2,1,0:T(8,128)} async-done(((f32[2,1024,256]{2,1,0:T(8,128)}), f32[2,1024,256]{2,1,0:T(8,128)}) %all-reduce.82.cloned.1.call-update) | async-done | bytes 2097168 | tf_op jit(solution)/shard_map/psum | solution.py:112
  1198.7 3.0 copy.438
  (805 shorter events, 230.4 us)
Async XLA Ops:
  7.2 96.3 %reduce-scatter.7.cloned.1.call-start = ((), (), s32[]{:S(2)}) async-start(), calls=%async_computation.6 | async-start | bytes 5242880 | tf_op jit(solution)/shard_map/reduce_scatter | solution.py:162
  8.1 285.1 %copy-start.117 = (f32[1,1024]{1,0:T(1,128)}, f32[1,1024]{1,0:T(1,128)S(1)}, u32[]{:S(2)}) copy-start(f32[1,1024]{1,0:T(1,128)S(1)} %get-tuple-element.187) | copy-start | bytes 12292
  11.1 49.3 %copy-start.56 = (bf16[256,1024]{1,0:T(8,128)(2,1)}, bf16[256,1024]{1,0:T(8,128)(2,1)S(1)}, u32[]{:S(2)}) copy-start(bf16[256,1024]{1,0:T(8,128)(2,1)S(1)} %fusion.68) | copy-start | bytes 1572868
  25.5 45.5 %copy-start.227 = (f32[2,128]{1,0:T(2,128)S(1)}, f32[2,128]{1,0:T(2,128)}, u32[]{:S(2)}) copy-start(f32[2,128]{1,0:T(2,128)} %param.25) | copy-start | bytes 3076
  25.5 46.1 %copy-start.228 = (f32[2,2]{1,0:T(2,128)S(1)}, f32[2,2]{1,0:T(2,128)}, u32[]{:S(2)}) copy-start(f32[2,2]{1,0:T(2,128)} %param.30) | copy-start | bytes 52
  25.5 46.6 %copy-start.221 = (f32[2,256]{1,0:T(2,128)S(1)}, f32[2,256]{1,0:T(2,128)}, u32[]{:S(2)}) copy-start(f32[2,256]{1,0:T(2,128)} %param.27) | copy-start | bytes 6148
  25.5 47.1 %copy-start.207 = (f32[2,4,128]{2,1,0:T(4,128)S(1)}, f32[2,4,128]{2,1,0:T(4,128)}, u32[]{:S(2)}) copy-start(f32[2,4,128]{2,1,0:T(4,128)} %param.24) | copy-start | bytes 12292
  25.5 49.8 %copy-start.173 = (f32[2,4,256]{2,1,0:T(4,128)S(1)}, f32[2,4,256]{2,1,0:T(4,128)}, u32[]{:S(2)}) copy-start(f32[2,4,256]{2,1,0:T(4,128)} %param.26) | copy-start | bytes 24580
  25.5 237.3 %reduce-scatter.9.cloned.1.call-start = ((), (), s32[]{:S(2)}) async-start(), calls=%async_computation.7 | async-start | bytes 4456448 | tf_op jit(solution)/shard_map/reduce_scatter | solution.py:189
  49.6 69.5 %copy-start.101 = (f32[1,1024,2]{1,2,0:T(2,128)}, f32[1,1024,2]{1,2,0:T(2,128)S(1)}, u32[]{:S(2)}) copy-start(f32[1,1024,2]{1,2,0:T(2,128)S(1)} %compare_select_fusion.5) | copy-start | bytes 24580
  70.9 47.1 %copy-start.166 = (f32[2]{0:T(128)}, f32[2]{0:T(128)S(1)}, u32[]{:S(2)}) copy-start(f32[2]{0:T(128)S(1)} %get-tuple-element.56) | copy-start | bytes 28
  70.9 47.1 %copy-start.190 = (f32[2]{0:T(128)}, f32[2]{0:T(128)S(1)}, u32[]{:S(2)}) copy-start(f32[2]{0:T(128)S(1)} %get-tuple-element.55) | copy-start | bytes 28
  73.2 37.2 %copy-start.174 = (f32[128]{0:T(128)}, f32[128]{0:T(128)S(1)}, u32[]{:S(2)}) copy-start(f32[128]{0:T(128)S(1)} %get-tuple-element.201) | copy-start | bytes 1540
  73.2 37.2 %copy-start.176 = (f32[128]{0:T(128)}, f32[128]{0:T(128)S(1)}, u32[]{:S(2)}) copy-start(f32[128]{0:T(128)S(1)} %get-tuple-element.198) | copy-start | bytes 1540
  73.2 37.2 %copy-start.178 = (f32[128]{0:T(128)}, f32[128]{0:T(128)S(1)}, u32[]{:S(2)}) copy-start(f32[128]{0:T(128)S(1)} %get-tuple-element.199) | copy-start | bytes 1540
  73.2 37.2 %copy-start.180 = (f32[128]{0:T(128)}, f32[128]{0:T(128)S(1)}, u32[]{:S(2)}) copy-start(f32[128]{0:T(128)S(1)} %get-tuple-element.200) | copy-start | bytes 1540
  75.3 285.1 %copy-start.105 = (f32[4,256]{1,0:T(4,128)}, f32[4,256]{1,0:T(4,128)S(1)}, u32[]{:S(2)}) copy-start(f32[4,256]{1,0:T(4,128)S(1)} %compare_convert_fusion.6) | copy-start | bytes 12292
  75.3 43.8 %copy-start.129 = (f32[256,2]{0,1:T(2,128)}, f32[256,2]{0,1:T(2,128)S(1)}, u32[]{:S(2)}) copy-start(f32[256,2]{0,1:T(2,128)S(1)} %get-tuple-element.189) | copy-start | bytes 6148
  75.3 43.8 %copy-start.131 = (f32[256,2]{0,1:T(2,128)}, f32[256,2]{0,1:T(2,128)S(1)}, u32[]{:S(2)}) copy-start(f32[256,2]{0,1:T(2,128)S(1)} %get-tuple-element.190) | copy-start | bytes 6148
  75.3 43.8 %copy-start.133 = (f32[256,2]{0,1:T(2,128)}, f32[256,2]{0,1:T(2,128)S(1)}, u32[]{:S(2)}) copy-start(f32[256,2]{0,1:T(2,128)S(1)} %get-tuple-element.191) | copy-start | bytes 6148
  76.0 316.3 %copy-start.89 = (f32[1,1024]{1,0:T(1,128)}, f32[1,1024]{1,0:T(1,128)S(1)}, u32[]{:S(2)}) copy-start(f32[1,1024]{1,0:T(1,128)S(1)} %get-tuple-element.207) | copy-start | bytes 12292
  76.0 316.3 %copy-start.92 = (f32[1,1024]{1,0:T(1,128)}, f32[1,1024]{1,0:T(1,128)S(1)}, u32[]{:S(2)}) copy-start(f32[1,1024]{1,0:T(1,128)S(1)} %get-tuple-element.208) | copy-start | bytes 12292
  76.1 316.3 %copy-start.95 = (f32[1,1024]{1,0:T(1,128)}, f32[1,1024]{1,0:T(1,128)S(1)}, u32[]{:S(2)}) copy-start(f32[1,1024]{1,0:T(1,128)S(1)} %get-tuple-element.209) | copy-start | bytes 12292
  76.2 41.1 %copy-start.111 = (f32[4,256,2]{1,2,0:T(2,128)}, f32[4,256,2]{1,2,0:T(2,128)S(1)}, u32[]{:S(2)}) copy-start(f32[4,256,2]{1,2,0:T(2,128)S(1)} %multiply_bitcast_fusion.7) | copy-start | bytes 24580
  79.5 37.8 %copy-start.4 = (f32[1,1024,128]{2,1,0:T(8,128)}, f32[1,1024,128]{2,1,0:T(8,128)S(1)}, u32[]{:S(2)}) copy-start(f32[1,1024,128]{2,1,0:T(8,128)S(1)} %get-tuple-element.150) | copy-start | bytes 1572868
  79.5 39.3 %copy-start.13 = (f32[1,1024,128]{2,1,0:T(8,128)}, f32[1,1024,128]{2,1,0:T(8,128)S(1)}, u32[]{:S(2)}) copy-start(f32[1,1024,128]{2,1,0:T(8,128)S(1)} %get-tuple-element.151) | copy-start | bytes 1572868
  119.2 45.6 %copy-start.224 = (f32[2,64]{1,0:T(2,128)S(1)}, f32[2,64]{1,0:T(2,128)}, u32[]{:S(2)}) copy-start(f32[2,64]{1,0:T(2,128)} %mul.2202) | copy-start | bytes 1540
  119.2 47.0 %copy-start.81 = (bf16[2,128,1024]{2,1,0:T(8,128)(2,1)S(1)}, bf16[2,128,1024]{2,1,0:T(8,128)(2,1)}, u32[]{:S(2)}) copy-start(bf16[2,128,1024]{2,1,0:T(8,128)(2,1)} %param.32) | copy-start | bytes 1572868
  169.0 122.1 %copy-start.2 = (bf16[256,1024]{1,0:T(8,128)(2,1)S(1)}, bf16[256,1024]{1,0:T(8,128)(2,1)}, u32[]{:S(2)}) copy-start(bf16[256,1024]{1,0:T(8,128)(2,1)} %param.17) | copy-start | bytes 1572868
  169.0 122.0 %all-gather.9.cloned.1.call-start = ((), (), s32[]{:S(2)}) async-start(), calls=%async_computation.8 | async-start | bytes 1310720 | tf_op jit(solution)/shard_map/all_gather | solution.py:195
  262.8 122.6 %reduce-scatter.11.cloned.1.call-start = ((), (), s32[]{:S(2)}) async-start(), calls=%async_computation.9 | async-start | bytes 5242880 | tf_op jit(solution)/shard_map/reduce_scatter | solution.py:162
  308.5 36.7 %copy-start.197 = (f32[2]{0:T(128)S(1)}, f32[2]{0:T(128)}, u32[]{:S(2)}) copy-start(f32[2]{0:T(128)} %get-tuple-element.228) | copy-start | bytes 28
  308.6 36.8 %copy-start.195 = (f32[2]{0:T(128)S(1)}, f32[2]{0:T(128)}, u32[]{:S(2)}) copy-start(f32[2]{0:T(128)} %get-tuple-element.226) | copy-start | bytes 28
  308.6 40.7 %copy-start.62 = (bf16[256,1024]{1,0:T(8,128)(2,1)S(1)}, bf16[256,1024]{1,0:T(8,128)(2,1)}, u32[]{:S(2)}) copy-start(bf16[256,1024]{1,0:T(8,128)(2,1)} %copy-done.61) | copy-start | bytes 1572868
  308.6 295.0 %all-gather.13.cloned.1.call-start = ((), (), s32[]{:S(2)}) async-start(), calls=%async_computation.12 | async-start | bytes 2621440 | tf_op jit(solution)/shard_map/all_gather | solution.py:242
  309.6 11.7 collective-permute-start
  311.4 48.3 %copy-start.141 = (f32[1,1,256]{2,1,0:T(1,128)S(1)}, f32[1,1,256]{2,1,0:T(1,128)}, u32[]{:S(2)}) copy-start(f32[1,1,256]{2,1,0:T(1,128)} %copy-done.140) | copy-start | bytes 3076
  311.4 48.3 %copy-start.143 = (f32[1,1,256]{2,1,0:T(1,128)S(1)}, f32[1,1,256]{2,1,0:T(1,128)}, u32[]{:S(2)}) copy-start(f32[1,1,256]{2,1,0:T(1,128)} %copy-done.142) | copy-start | bytes 3076
  311.4 48.3 %copy-start.145 = (f32[1,1,256]{2,1,0:T(1,128)S(1)}, f32[1,1,256]{2,1,0:T(1,128)}, u32[]{:S(2)}) copy-start(f32[1,1,256]{2,1,0:T(1,128)} %copy-done.144) | copy-start | bytes 3076
  323.9 132.1 %collective-permute-start.1 = (bf16[512,1024]{1,0:T(8,128)(2,1)}, bf16[512,1024]{1,0:T(8,128)(2,1)}, u32[]{:S(2)}, u32[]{:S(2)}) collective-permute-start(bf16[512,1024]{1,0:T(8,128)(2,1)} %maximum_select_fusion.2), channel_id=1, source_target_pairs={{0,8},{4,12},{8,0},{12,4},{1,9},{5,13},{9,1},{13,5},{2,10},{6,14},... | collective-permute-start | bytes 3145736 | tf_op jit(solution)/shard_map/ppermute | solution.py:210
  325.2 35.4 %copy-start.158 = (f32[1,1,256]{2,1,0:T(1,128)S(1)}, f32[1,1,256]{2,1,0:T(1,128)}, u32[]{:S(2)}) copy-start(f32[1,1,256]{2,1,0:T(1,128)} %get-tuple-element.186) | copy-start | bytes 3076
  325.2 35.4 %copy-start.160 = (f32[1,1,256]{2,1,0:T(1,128)S(1)}, f32[1,1,256]{2,1,0:T(1,128)}, u32[]{:S(2)}) copy-start(f32[1,1,256]{2,1,0:T(1,128)} %get-tuple-element.180) | copy-start | bytes 3076
  325.2 35.4 %copy-start.164 = (f32[1,1,256]{2,1,0:T(1,128)S(1)}, f32[1,1,256]{2,1,0:T(1,128)}, u32[]{:S(2)}) copy-start(f32[1,1,256]{2,1,0:T(1,128)} %get-tuple-element.179) | copy-start | bytes 3076
  325.2 35.4 %copy-start.199 = (f32[1,256]{1,0:T(1,128)S(1)}, f32[1,256]{1,0:T(1,128)}, u32[]{:S(2)}) copy-start(f32[1,256]{1,0:T(1,128)} %get-tuple-element.210) | copy-start | bytes 3076
  359.8 42.6 %copy-start.168 = (f32[2]{0:T(128)}, f32[2]{0:T(128)S(1)}, u32[]{:S(2)}) copy-start(f32[2]{0:T(128)S(1)} %get-tuple-element.54) | copy-start | bytes 28
  359.8 42.6 %copy-start.192 = (f32[2]{0:T(128)}, f32[2]{0:T(128)S(1)}, u32[]{:S(2)}) copy-start(f32[2]{0:T(128)S(1)} %get-tuple-element.53) | copy-start | bytes 28
  360.5 39.8 %copy-start.113 = (f32[4,256,2]{1,2,0:T(2,128)}, f32[4,256,2]{1,2,0:T(2,128)S(1)}, u32[]{:S(2)}) copy-start(f32[4,256,2]{1,2,0:T(2,128)S(1)} %multiply_bitcast_fusion.6) | copy-start | bytes 24580
  540.3 52.0 %copy-start.80 = (f32[1,1,2,128,64]{3,4,2,1,0:T(8,128)S(1)}, f32[1,1,2,128,64]{3,4,2,1,0:T(8,128)}, u32[]{:S(2)}) copy-start(f32[1,1,2,128,64]{3,4,2,1,0:T(8,128)} %copy-done.79) | copy-start | bytes 196612
  541.1 52.6 %copy-start.78 = (f32[1,1,2,128,64]{3,4,2,1,0:T(8,128)S(1)}, f32[1,1,2,128,64]{3,4,2,1,0:T(8,128)}, u32[]{:S(2)}) copy-start(f32[1,1,2,128,64]{3,4,2,1,0:T(8,128)} %copy-done.77) | copy-start | bytes 196612
  541.1 55.2 %copy-start.8 = (f32[1,1024,128]{2,1,0:T(8,128)S(1)}, f32[1,1024,128]{2,1,0:T(8,128)}, u32[]{:S(2)}) copy-start(f32[1,1024,128]{2,1,0:T(8,128)} %copy-done.6) | copy-start | bytes 1572868
  542.0 91.6 %reduce-scatter.15.cloned.1.call-start = ((), (), s32[]{:S(2)}) async-start(), calls=%async_computation.13 | async-start | bytes 1310720 | tf_op jit(solution)/shard_map/reduce_scatter | solution.py:269
  607.7 125.5 %reduce-scatter.13.cloned.1.call-start = ((), (), s32[]{:S(2)}) async-start(), calls=%async_computation.10 | async-start | bytes 4456448 | tf_op jit(solution)/shard_map/reduce_scatter | solution.py:189
  611.0 150.5 %all-gather.15.cloned.1.call-start = ((), (), s32[]{:S(2)}) async-start(), calls=%async_computation.14 | async-start | bytes 1310720 | tf_op jit(solution)/shard_map/all_gather | solution.py:277
  633.6 156.8 %all-gather.11.cloned.1.call-start = ((), (), s32[]{:S(2)}) async-start(), calls=%async_computation.11 | async-start | bytes 1310720 | tf_op jit(solution)/shard_map/all_gather | solution.py:195
  733.2 242.0 %all-gather.17.cloned.1.call-start = ((), (), s32[]{:S(2)}) async-start(), calls=%async_computation.15 | async-start | bytes 2621440 | tf_op jit(solution)/shard_map/all_gather | solution.py:242
  793.6 13.2 %collective-permute-start.2 = (bf16[256,1024]{1,0:T(8,128)(2,1)S(1)}, bf16[256,1024]{1,0:T(8,128)(2,1)S(1)}, u32[]{:S(2)}, u32[]{:S(2)}) collective-permute-start(bf16[256,1024]{1,0:T(8,128)(2,1)S(1)} %get-tuple-element.110), channel_id=1, source_target_pairs={{0,4},{4,0},{8,12},{12,8},{1,5},{5,1},{9,13},{13,9},{2,6},{6,2},{1... | collective-permute-start | bytes 1572872 | tf_op jit(solution)/shard_map/ppermute | solution.py:210
  808.2 23.9 %collective-permute-start.3 = (bf16[512,1024]{1,0:T(8,128)(2,1)}, bf16[512,1024]{1,0:T(8,128)(2,1)}, u32[]{:S(2)}, u32[]{:S(2)}) collective-permute-start(bf16[512,1024]{1,0:T(8,128)(2,1)} %maximum_select_fusion.3), channel_id=1, source_target_pairs={{0,8},{4,12},{8,0},{12,4},{1,9},{5,13},{9,1},{13,5},{2,10},{6,14},... | collective-permute-start | bytes 3145736 | tf_op jit(solution)/shard_map/ppermute | solution.py:210
  913.2 51.1 %copy-start.25 = (f32[1,4,256,2,64]{2,4,3,1,0:T(8,128)S(1)}, f32[1,4,256,2,64]{2,4,3,1,0:T(8,128)}, u32[]{:S(2)}) copy-start(f32[1,4,256,2,64]{2,4,3,1,0:T(8,128)} %copy-done.24) | copy-start | bytes 1572868
  914.1 89.8 %reduce-scatter.17.cloned.1.call-start = ((), (), s32[]{:S(2)}) async-start(), calls=%async_computation.16 | async-start | bytes 1310720 | tf_op jit(solution)/shard_map/reduce_scatter | solution.py:269
  979.3 54.1 %all-gather.19.cloned.1.call-start = ((), (), s32[]{:S(2)}) async-start(), calls=%async_computation.17 | async-start | bytes 1310720 | tf_op jit(solution)/shard_map/all_gather | solution.py:277
  1003.9 52.8 %all-reduce.84.cloned.1.call-start = ((), (), s32[]{:S(2)}) async-start(), calls=%async_computation.19 | async-start | bytes 3145728 | tf_op jit(solution)/shard_map/psum | solution.py:108
  1014.0 184.6 %all-reduce.82.cloned.1.call-start = ((), (), s32[]{:S(2)}) async-start(), calls=%async_computation.18 | async-start | bytes 4194304 | tf_op jit(solution)/shard_map/psum | solution.py:112
  1060.8 43.3 %copy-start.38 = (f32[256,1024]{1,0:T(8,128)S(1)}, f32[256,1024]{1,0:T(8,128)}, u32[]{:S(2)}) copy-start(f32[256,1024]{1,0:T(8,128)} %get-tuple-element.111) | copy-start | bytes 3145732
  1060.9 43.3 %copy-start.198 = (f32[256]{0:T(256)S(1)}, f32[256]{0:T(256)}, u32[]{:S(2)}) copy-start(f32[256]{0:T(256)} %get-tuple-element.214) | copy-start | bytes 3076
  (196 other events, 1133.0 us)
Sparse Core Ops, SparseCore 0:
  25.6 77.8 reduce-scatter.6
  169.1 93.6 reduce-scatter.8
  264.4 26.6 all-gather.8
  308.7 76.6 reduce-scatter.10
  542.1 43.7 all-gather.12
  607.8 25.7 reduce-scatter.14
  635.9 97.3 reduce-scatter.12
  734.8 26.6 all-gather.14
  763.0 27.3 all-gather.10
  914.2 42.2 all-gather.16
  979.4 24.3 reduce-scatter.16
  1005.3 28.0 all-gather.18
  1036.9 19.7 all-reduce.83
  1062.5 136.1 all-reduce.81
